TPU v7x, 32 devices: a whole 2x2x4 slice. The times are simulated.
32 devices in a mesh: ray: 4 (over y, core), cuts: 8 (over z, x).
Axes of the slice: x: 2, y: 2, z: 4, core: 2. Of those that a mesh axis runs over, the one named last changes fastest.
Arguments:
- initial: float32 [16, 16, 4096], P('cuts', 'ray'), may hold values from 0.5 to 1.5
- measured: float32 [4, 32, 16, 4096], P('ray', None, 'cuts'), may hold values from 9.6 to 28.8
- order: int32 [4], replicated, may hold values from 0 to 3, each once
- angle_index: int32 [4, 32], replicated, may hold values from 0 to 2999
Outputs:
- reconstruction: float32 [16, 16, 4096], P('cuts', 'ray')
Inputs may be any that keep to these rules, and one draw needn't show every extreme that they name: Each stored subset appears once; the first 2 entries are the subsets run, in order, and stored subset j is held by index j of ray.
All inputs are finite; a program needn't handle non-finite values.
Results may differ from a plain program's by a relative error of at most 0.0003.
Values sent between devices are 32-bit elements; how exact they have to be, the bound alone decides.
No kernel may reach another device: no remote copies, remote signals or barrier semaphores. Data moves between devices by JAX's collectives and lax.ppermute only.
A program may use at most 64 MiB of HBM per device.

v0:
```python
import jax
import jax.numpy as jnp
from jax import lax
from jax.sharding import PartitionSpec as P

SUBSETS = 2
NANG = 3000
TV_ITERS = 2
TV_STEP = 0.05
TV_EPS = 0.5
angle_group = 2


def broadcast(value, axis, source):
    kept = jnp.where(lax.axis_index(axis) == source, value, 0).astype(value.dtype)
    return lax.psum(kept, axis)


def padded_2(block, sides, width):
    for axis, dim in sides:
        count = lax.axis_size(axis)
        forward = [(i, i + 1) for i in range(count - 1)]
        backward = [(target, source) for source, target in forward]
        low = lax.ppermute(
            lax.slice_in_dim(block, block.shape[dim] - width, None, axis=dim), axis, forward
        )
        high = lax.ppermute(lax.slice_in_dim(block, 0, width, axis=dim), axis, backward)
        block = jnp.concatenate([low, block, high], axis=dim)
    return block


def strip_geometry(angle_row, first_row, total_rows, strip_rows):
    slopes = -1.0 + (2.0 * angle_row.astype(jnp.float32) + 1.0) / NANG
    row_pos = (first_row + jnp.arange(strip_rows, dtype=jnp.int32)).astype(jnp.float32) - (
        total_rows - 1
    ) / 2.0
    spread = slopes[:, None] * row_pos[None, :]
    floor_part = jnp.floor(spread)
    return (floor_part.astype(jnp.int32), spread - floor_part)


def row_windows(padded, starts, width):

    def row_one_row(plane, start):
        return lax.dynamic_slice_in_dim(plane, start, width, 1)

    return jax.vmap(row_one_row, in_axes=(1, 0), out_axes=1)(padded, starts)


def plane_windows(plane, starts, width):

    def plane_one_row(start):
        return lax.dynamic_slice_in_dim(plane, start, width, 1)

    return jax.vmap(plane_one_row, out_axes=1)(starts)


def project_block(padded, shifts, fraction, margin, width):
    angle_count, rows = shifts.shape
    groups = angle_count // angle_group

    def project_one_angle(shift_row, frac_row):
        window = row_windows(padded, margin - shift_row - 1, width + 1)
        weight = frac_row[None, :, None]
        return jnp.sum((1.0 - weight) * window[:, :, 1:] + weight * window[:, :, :-1], axis=1)

    def one_group(pieces):
        return jax.vmap(project_one_angle)(pieces[0], pieces[1])

    result = lax.map(
        one_group,
        (shifts.reshape(groups, angle_group, rows), fraction.reshape(groups, angle_group, rows)),
    )
    return result.reshape(angle_count, padded.shape[0], width)


def back_block(res_padded, shifts, fraction, margin, width):
    angle_count, rows = shifts.shape
    groups = angle_count // angle_group
    slices = res_padded.shape[1]

    def back_one_angle(plane, shift_row, frac_row):
        window = plane_windows(plane, margin + shift_row, width + 1)
        weight = frac_row[None, :, None]
        return (1.0 - weight) * window[:, :, :-1] + weight * window[:, :, 1:]

    def add_group(summed, pieces):
        terms = jax.vmap(back_one_angle)(pieces[0], pieces[1], pieces[2])
        return (summed + jnp.sum(terms, axis=0), None)

    planes = res_padded.reshape((groups, angle_group) + res_padded.shape[1:])
    summed, _ = lax.scan(
        add_group,
        jnp.zeros((slices, rows, width), jnp.float32),
        (
            planes,
            shifts.reshape(groups, angle_group, rows),
            fraction.reshape(groups, angle_group, rows),
        ),
    )
    return summed


def tv_step(extended, first_row, first_slice, total_rows, total_slices):
    count_s, count_r, breadth = extended.shape
    row_ids = first_row + jnp.arange(count_r, dtype=jnp.int32)
    slice_ids = first_slice + jnp.arange(count_s, dtype=jnp.int32)
    row_in = (row_ids >= 0) & (row_ids < total_rows)
    slice_in = (slice_ids >= 0) & (slice_ids < total_slices)
    centre = extended[:-1, :-1]
    cell_in = slice_in[:-1, None] & row_in[None, :-1]
    valid_r = cell_in & row_in[None, 1:]
    valid_s = cell_in & slice_in[1:, None]
    step_r = jnp.where(valid_r[:, :, None], extended[:-1, 1:] - centre, 0.0)
    step_s = jnp.where(valid_s[:, :, None], extended[1:, :-1] - centre, 0.0)
    along_c = jnp.concatenate(
        [centre[:, :, 1:] - centre[:, :, :-1], jnp.zeros_like(centre[:, :, :1])], axis=2
    )
    step_c = jnp.where(cell_in[:, :, None], along_c, 0.0)
    magnitude = jnp.sqrt(step_s * step_s + step_r * step_r + step_c * step_c + TV_EPS * TV_EPS)
    flow_r = step_r / magnitude
    flow_s = step_s / magnitude
    flow_c = step_c / magnitude
    inner_c = flow_c[1:, 1:]
    spread = flow_r[1:, 1:] - flow_r[1:, :-1] + flow_s[1:, 1:] - flow_s[:-1, 1:]
    spread = spread + inner_c - jnp.pad(inner_c[:, :, :-1], ((0, 0), (0, 0), (1, 0)))
    return extended[1:-1, 1:-1] + TV_STEP * spread


def on_device(initial, measured, order, angle_index):
    slices, strip_rows, breadth = initial.shape
    ray_count = lax.axis_size("ray")
    cut_count = lax.axis_size("cuts")
    ray_place = lax.axis_index("ray")
    cut_place = lax.axis_index("cuts")
    total_rows = strip_rows * ray_count
    total_slices = slices * cut_count
    angle_total = angle_index.shape[1]
    margin = total_rows // 2 + 2
    stored = measured[0]
    current = initial
    for subset in range(SUBSETS):
        subset_slot = order[subset]
        shifts, fraction = strip_geometry(
            angle_index[subset_slot], ray_place * strip_rows, total_rows, strip_rows
        )
        padded = jnp.pad(current, ((0, 0), (0, 0), (margin, margin)))
        partial_value = project_block(padded, shifts, fraction, margin, breadth)
        totals = lax.psum(partial_value, "ray")
        residual = broadcast(stored - totals, "ray", subset_slot)
        res_padded = jnp.pad(residual, ((0, 0), (0, 0), (margin, margin)))
        current = current + back_block(res_padded, shifts, fraction, margin, breadth) / (
            total_rows * angle_total
        )
        for tv_turn in range(TV_ITERS):
            extended = padded_2(current, (("ray", 1), ("cuts", 0)), 1)
            current = tv_step(
                extended,
                ray_place * strip_rows - 1,
                cut_place * slices - 1,
                total_rows,
                total_slices,
            )
    return current


def solution(mesh):
    return jax.shard_map(
        on_device,
        mesh=mesh,
        in_specs=(P("cuts", "ray", None), P("ray", None, "cuts", None), P(), P()),
        out_specs=P("cuts", "ray", None),
        check_vma=False,
    )
```

profile of v0, /device:TPU:1, one launch (start us, length us, event | category | flops | bytes accessed | tf_op | source)
XLA Modules:
  0.0 1349.5 jit_solution(12900914432349245809)
XLA Ops:
  14.4 270.8 %while.65 = (s32[]{:T(128)}, f32[16,2,2,4096]{3,2,1,0:T(2,128)S(1)}, f32[16,2,4]{2,1,0:T(2,128)S(1)}, f32[2,4,4116]{2,0,1:T(2,128)S(1)}, s32[16,2,4]{2,1,0:T(2,128)S(1)}, /*index=5*/s32[]{:T(128)}, s32[]{:T(128)}, s32[]{:T(128)}) while((s32[]{:T(128)}, f32[16,2,2,4096]{3,2,1,0:T(2,128)S(1)}, f32[16,2,4]{2,1,0:T(2,128)S(1)}, ...), condition=%wide.region_2.3_spmd, body=%wide.region_0.2_spmd.sunk | while | flops 245828 | bytes 789350 | solution.py:70
  287.0 37.4 %all-reduce.21.cloned.1.call-done = f32[32,2,4096]{2,1,0:T(2,128)} async-done(((f32[32,2,4096]{2,1,0:T(2,128)}), f32[32,2,4096]{2,1,0:T(2,128)}) %all-reduce.21.cloned.1.call-update) | async-done | bytes 1048592 | tf_op jit(solution)/shard_map/psum | solution.py:149
  327.6 36.7 %all-reduce.23.cloned.1.call-done = f32[32,2,4096]{2,1,0:T(2,128)} async-done(((f32[32,2,4096]{2,1,0:T(2,128)}), f32[32,2,4096]{2,1,0:T(2,128)}) %all-reduce.23.cloned.1.call-update) | async-done | bytes 1048592 | tf_op jit(solution)/shard_map/psum | solution.py:16
  366.7 274.4 %while.69 = (s32[]{:T(128)}, f32[2,4,4096]{2,0,1:T(2,128)S(1)}, f32[16,2,4]{2,1,0:T(2,128)S(1)}, f32[16,2,2,4116]{3,2,1,0:T(2,128)S(1)}, s32[16,2,4]{2,1,0:T(2,128)S(1)}, /*index=5*/s32[]{:T(128)}, s32[]{:T(128)}, s32[]{:T(128)}) while((s32[]{:T(128)}, f32[2,4,4096]{2,0,1:T(2,128)S(1)}, f32[16,2,4]{2,1,0:T(2,128)S(1)}, ...), condition=%wide.region_7.8_spmd.clone, body=%wide.region_5.7_spmd.clone.sunk | while | flops 294981 | bytes 1248752 | solution.py:92
  366.8 16.3 %while.74 = (s32[]{:T(128)}, f32[2,2,4116]{2,1,0:T(2,128)S(1)}, s32[8,3]{0,1:T(4,128)S(1)}, f32[8,2,4097]{2,1,0:T(2,128)S(1)}, s32[]{:T(128)}) while((s32[]{:T(128)}, f32[2,2,4116]{2,1,0:T(2,128)S(1)}, s32[8,3]{0,1:T(4,128)S(1)}, f32[8,2,4097]{2,1,0:T(2,128)S(1)}, s32[]{:T(128)}) %tuple.230), condition=%wide.while_cond.1, body=%wide.while_body.1.sunk | while | flops 2 | bytes 67701 | solution.py:53
  384.0 16.3 %while.74 = (s32[]{:T(128)}, f32[2,2,4116]{2,1,0:T(2,128)S(1)}, s32[8,3]{0,1:T(4,128)S(1)}, f32[8,2,4097]{2,1,0:T(2,128)S(1)}, s32[]{:T(128)}) while((s32[]{:T(128)}, f32[2,2,4116]{2,1,0:T(2,128)S(1)}, s32[8,3]{0,1:T(4,128)S(1)}, f32[8,2,4097]{2,1,0:T(2,128)S(1)}, s32[]{:T(128)}) %tuple.230), condition=%wide.while_cond.1, body=%wide.while_body.1.sunk | while | flops 2 | bytes 67701 | solution.py:53
  401.1 16.3 %while.74 = (s32[]{:T(128)}, f32[2,2,4116]{2,1,0:T(2,128)S(1)}, s32[8,3]{0,1:T(4,128)S(1)}, f32[8,2,4097]{2,1,0:T(2,128)S(1)}, s32[]{:T(128)}) while((s32[]{:T(128)}, f32[2,2,4116]{2,1,0:T(2,128)S(1)}, s32[8,3]{0,1:T(4,128)S(1)}, f32[8,2,4097]{2,1,0:T(2,128)S(1)}, s32[]{:T(128)}) %tuple.230), condition=%wide.while_cond.1, body=%wide.while_body.1.sunk | while | flops 2 | bytes 67701 | solution.py:53
  435.4 16.3 %while.74 = (s32[]{:T(128)}, f32[2,2,4116]{2,1,0:T(2,128)S(1)}, s32[8,3]{0,1:T(4,128)S(1)}, f32[8,2,4097]{2,1,0:T(2,128)S(1)}, s32[]{:T(128)}) while((s32[]{:T(128)}, f32[2,2,4116]{2,1,0:T(2,128)S(1)}, s32[8,3]{0,1:T(4,128)S(1)}, f32[8,2,4097]{2,1,0:T(2,128)S(1)}, s32[]{:T(128)}) %tuple.230), condition=%wide.while_cond.1, body=%wide.while_body.1.sunk | while | flops 2 | bytes 67701 | solution.py:53
  452.6 16.3 %while.74 = (s32[]{:T(128)}, f32[2,2,4116]{2,1,0:T(2,128)S(1)}, s32[8,3]{0,1:T(4,128)S(1)}, f32[8,2,4097]{2,1,0:T(2,128)S(1)}, s32[]{:T(128)}) while((s32[]{:T(128)}, f32[2,2,4116]{2,1,0:T(2,128)S(1)}, s32[8,3]{0,1:T(4,128)S(1)}, f32[8,2,4097]{2,1,0:T(2,128)S(1)}, s32[]{:T(128)}) %tuple.230), condition=%wide.while_cond.1, body=%wide.while_body.1.sunk | while | flops 2 | bytes 67701 | solution.py:53
  469.7 16.3 %while.74 = (s32[]{:T(128)}, f32[2,2,4116]{2,1,0:T(2,128)S(1)}, s32[8,3]{0,1:T(4,128)S(1)}, f32[8,2,4097]{2,1,0:T(2,128)S(1)}, s32[]{:T(128)}) while((s32[]{:T(128)}, f32[2,2,4116]{2,1,0:T(2,128)S(1)}, s32[8,3]{0,1:T(4,128)S(1)}, f32[8,2,4097]{2,1,0:T(2,128)S(1)}, s32[]{:T(128)}) %tuple.230), condition=%wide.while_cond.1, body=%wide.while_body.1.sunk | while | flops 2 | bytes 67701 | solution.py:53
  504.0 16.3 %while.74 = (s32[]{:T(128)}, f32[2,2,4116]{2,1,0:T(2,128)S(1)}, s32[8,3]{0,1:T(4,128)S(1)}, f32[8,2,4097]{2,1,0:T(2,128)S(1)}, s32[]{:T(128)}) while((s32[]{:T(128)}, f32[2,2,4116]{2,1,0:T(2,128)S(1)}, s32[8,3]{0,1:T(4,128)S(1)}, f32[8,2,4097]{2,1,0:T(2,128)S(1)}, s32[]{:T(128)}) %tuple.230), condition=%wide.while_cond.1, body=%wide.while_body.1.sunk | while | flops 2 | bytes 67701 | solution.py:53
  521.2 16.3 %while.74 = (s32[]{:T(128)}, f32[2,2,4116]{2,1,0:T(2,128)S(1)}, s32[8,3]{0,1:T(4,128)S(1)}, f32[8,2,4097]{2,1,0:T(2,128)S(1)}, s32[]{:T(128)}) while((s32[]{:T(128)}, f32[2,2,4116]{2,1,0:T(2,128)S(1)}, s32[8,3]{0,1:T(4,128)S(1)}, f32[8,2,4097]{2,1,0:T(2,128)S(1)}, s32[]{:T(128)}) %tuple.230), condition=%wide.while_cond.1, body=%wide.while_body.1.sunk | while | flops 2 | bytes 67701 | solution.py:53
  538.3 16.3 %while.74 = (s32[]{:T(128)}, f32[2,2,4116]{2,1,0:T(2,128)S(1)}, s32[8,3]{0,1:T(4,128)S(1)}, f32[8,2,4097]{2,1,0:T(2,128)S(1)}, s32[]{:T(128)}) while((s32[]{:T(128)}, f32[2,2,4116]{2,1,0:T(2,128)S(1)}, s32[8,3]{0,1:T(4,128)S(1)}, f32[8,2,4097]{2,1,0:T(2,128)S(1)}, s32[]{:T(128)}) %tuple.230), condition=%wide.while_cond.1, body=%wide.while_body.1.sunk | while | flops 2 | bytes 67701 | solution.py:53
  572.6 16.3 %while.74 = (s32[]{:T(128)}, f32[2,2,4116]{2,1,0:T(2,128)S(1)}, s32[8,3]{0,1:T(4,128)S(1)}, f32[8,2,4097]{2,1,0:T(2,128)S(1)}, s32[]{:T(128)}) while((s32[]{:T(128)}, f32[2,2,4116]{2,1,0:T(2,128)S(1)}, s32[8,3]{0,1:T(4,128)S(1)}, f32[8,2,4097]{2,1,0:T(2,128)S(1)}, s32[]{:T(128)}) %tuple.230), condition=%wide.while_cond.1, body=%wide.while_body.1.sunk | while | flops 2 | bytes 67701 | solution.py:53
  589.8 16.3 %while.74 = (s32[]{:T(128)}, f32[2,2,4116]{2,1,0:T(2,128)S(1)}, s32[8,3]{0,1:T(4,128)S(1)}, f32[8,2,4097]{2,1,0:T(2,128)S(1)}, s32[]{:T(128)}) while((s32[]{:T(128)}, f32[2,2,4116]{2,1,0:T(2,128)S(1)}, s32[8,3]{0,1:T(4,128)S(1)}, f32[8,2,4097]{2,1,0:T(2,128)S(1)}, s32[]{:T(128)}) %tuple.230), condition=%wide.while_cond.1, body=%wide.while_body.1.sunk | while | flops 2 | bytes 67701 | solution.py:53
  606.9 16.3 %while.74 = (s32[]{:T(128)}, f32[2,2,4116]{2,1,0:T(2,128)S(1)}, s32[8,3]{0,1:T(4,128)S(1)}, f32[8,2,4097]{2,1,0:T(2,128)S(1)}, s32[]{:T(128)}) while((s32[]{:T(128)}, f32[2,2,4116]{2,1,0:T(2,128)S(1)}, s32[8,3]{0,1:T(4,128)S(1)}, f32[8,2,4097]{2,1,0:T(2,128)S(1)}, s32[]{:T(128)}) %tuple.230), condition=%wide.while_cond.1, body=%wide.while_body.1.sunk | while | flops 2 | bytes 67701 | solution.py:53
  624.0 16.3 %while.74 = (s32[]{:T(128)}, f32[2,2,4116]{2,1,0:T(2,128)S(1)}, s32[8,3]{0,1:T(4,128)S(1)}, f32[8,2,4097]{2,1,0:T(2,128)S(1)}, s32[]{:T(128)}) while((s32[]{:T(128)}, f32[2,2,4116]{2,1,0:T(2,128)S(1)}, s32[8,3]{0,1:T(4,128)S(1)}, f32[8,2,4097]{2,1,0:T(2,128)S(1)}, s32[]{:T(128)}) %tuple.230), condition=%wide.while_cond.1, body=%wide.while_body.1.sunk | while | flops 2 | bytes 67701 | solution.py:53
  680.0 270.8 %while.67 = (s32[]{:T(128)}, f32[16,2,2,4096]{3,2,1,0:T(2,128)S(1)}, f32[16,2,4]{2,1,0:T(2,128)S(1)}, f32[2,4,4116]{2,0,1:T(2,128)S(1)}, s32[16,2,4]{2,1,0:T(2,128)S(1)}, /*index=5*/s32[]{:T(128)}, s32[]{:T(128)}, s32[]{:T(128)}) while((s32[]{:T(128)}, f32[16,2,2,4096]{3,2,1,0:T(2,128)S(1)}, f32[16,2,4]{2,1,0:T(2,128)S(1)}, ...), condition=%wide.region_10.11_spmd, body=%wide.region_8.10_spmd.sunk | while | flops 245828 | bytes 789350 | solution.py:70
  952.5 35.1 %all-reduce.25.cloned.1.call-done = f32[32,2,4096]{2,1,0:T(2,128)} async-done(((f32[32,2,4096]{2,1,0:T(2,128)}), f32[32,2,4096]{2,1,0:T(2,128)}) %all-reduce.25.cloned.1.call-update) | async-done | bytes 1048592 | tf_op jit(solution)/shard_map/psum | solution.py:149
  990.5 36.9 %all-reduce.27.cloned.1.call-done = f32[32,2,4096]{2,1,0:T(2,128)} async-done(((f32[32,2,4096]{2,1,0:T(2,128)}), f32[32,2,4096]{2,1,0:T(2,128)}) %all-reduce.27.cloned.1.call-update) | async-done | bytes 1048592 | tf_op jit(solution)/shard_map/psum | solution.py:16
  1029.8 274.4 %while.71 = (s32[]{:T(128)}, f32[2,4,4096]{2,0,1:T(2,128)S(1)}, f32[16,2,4]{2,1,0:T(2,128)S(1)}, f32[16,2,2,4116]{3,2,1,0:T(2,128)S(1)}, s32[16,2,4]{2,1,0:T(2,128)S(1)}, /*index=5*/s32[]{:T(128)}, s32[]{:T(128)}, s32[]{:T(128)}) while((s32[]{:T(128)}, f32[2,4,4096]{2,0,1:T(2,128)S(1)}, f32[16,2,4]{2,1,0:T(2,128)S(1)}, ...), condition=%wide.region_15.16_spmd.clone, body=%wide.region_13.15_spmd.clone.sunk | while | flops 294981 | bytes 1248752 | solution.py:92
  1030.0 16.3 %while.75 = (s32[]{:T(128)}, f32[2,2,4116]{2,1,0:T(2,128)S(1)}, s32[8,3]{0,1:T(4,128)S(1)}, f32[8,2,4097]{2,1,0:T(2,128)S(1)}, s32[]{:T(128)}) while((s32[]{:T(128)}, f32[2,2,4116]{2,1,0:T(2,128)S(1)}, s32[8,3]{0,1:T(4,128)S(1)}, f32[8,2,4097]{2,1,0:T(2,128)S(1)}, s32[]{:T(128)}) %tuple.227), condition=%wide.while_cond.3, body=%wide.while_body.3.sunk | while | flops 2 | bytes 67701 | solution.py:53
  1047.1 16.3 %while.75 = (s32[]{:T(128)}, f32[2,2,4116]{2,1,0:T(2,128)S(1)}, s32[8,3]{0,1:T(4,128)S(1)}, f32[8,2,4097]{2,1,0:T(2,128)S(1)}, s32[]{:T(128)}) while((s32[]{:T(128)}, f32[2,2,4116]{2,1,0:T(2,128)S(1)}, s32[8,3]{0,1:T(4,128)S(1)}, f32[8,2,4097]{2,1,0:T(2,128)S(1)}, s32[]{:T(128)}) %tuple.227), condition=%wide.while_cond.3, body=%wide.while_body.3.sunk | while | flops 2 | bytes 67701 | solution.py:53
  1064.3 16.3 %while.75 = (s32[]{:T(128)}, f32[2,2,4116]{2,1,0:T(2,128)S(1)}, s32[8,3]{0,1:T(4,128)S(1)}, f32[8,2,4097]{2,1,0:T(2,128)S(1)}, s32[]{:T(128)}) while((s32[]{:T(128)}, f32[2,2,4116]{2,1,0:T(2,128)S(1)}, s32[8,3]{0,1:T(4,128)S(1)}, f32[8,2,4097]{2,1,0:T(2,128)S(1)}, s32[]{:T(128)}) %tuple.227), condition=%wide.while_cond.3, body=%wide.while_body.3.sunk | while | flops 2 | bytes 67701 | solution.py:53
  (2238 shorter events, 1953.1 us)
Async XLA Ops:
  6.5 317.9 %all-reduce.21.cloned.1.call-start = ((), (), s32[]{:S(2)}) async-start(), calls=%async_computation | async-start | bytes 2097152 | tf_op jit(solution)/shard_map/psum | solution.py:149
  285.3 1.0 copy-start.1
  285.3 39.1 %copy-start = (f32[1,32,2,4096]{3,2,1,0:T(2,128)S(1)}, f32[1,32,2,4096]{3,2,1,0:T(2,128)}, u32[]{:S(2)}) copy-start(f32[1,32,2,4096]{3,2,1,0:T(2,128)} %param.13) | copy-start | bytes 3145732
  286.3 78.0 %all-reduce.23.cloned.1.call-start = ((), (), s32[]{:S(2)}) async-start(), calls=%async_computation.1 | async-start | bytes 2097152 | tf_op jit(solution)/shard_map/psum | solution.py:16
  327.4 660.2 %all-reduce.25.cloned.1.call-start = ((), (), s32[]{:S(2)}) async-start(), calls=%async_computation.2 | async-start | bytes 2097152 | tf_op jit(solution)/shard_map/psum | solution.py:149
  366.7 274.4 %copy-start.3 = (f32[2,4,4096]{2,1,0:T(4,128)S(1)}, f32[2,4,4096]{2,1,0:T(4,128)}, u32[]{:S(2)}) copy-start(f32[2,4,4096]{2,1,0:T(4,128)} %param.12) | copy-start | bytes 393220
  641.2 5.6 collective-permute-start
  644.8 5.2 collective-permute-start.1
  650.2 5.0 collective-permute-start.2
  653.3 5.7 collective-permute-start.3
  659.9 5.3 collective-permute-start.4
  663.3 5.2 collective-permute-start.5
  668.6 5.9 collective-permute-start.6
  672.6 5.7 collective-permute-start.7
  950.9 1.0 copy-start.2
  951.9 75.6 %all-reduce.27.cloned.1.call-start = ((), (), s32[]{:S(2)}) async-start(), calls=%async_computation.3 | async-start | bytes 2097152 | tf_op jit(solution)/shard_map/psum | solution.py:16
  1304.4 5.5 collective-permute-start.8
  1307.9 5.2 collective-permute-start.9
  1313.3 5.0 collective-permute-start.10
  1316.4 5.7 collective-permute-start.11
  1323.1 5.3 collective-permute-start.12
  1326.4 5.2 collective-permute-start.13
  1331.7 5.9 collective-permute-start.14
  1335.8 5.7 collective-permute-start.15
Sparse Core Ops, SparseCore 0:
  286.4 37.9 all-reduce.20
  327.5 36.7 all-reduce.22
  952.0 35.5 all-reduce.24
  990.6 36.7 all-reduce.26
where the time goes:
time: 1360 us; the launch traced here: 1350 us
  local copies, waits for them, and re-layouts  1050 us (77%)
  waiting for transfers between devices  176 us (13%)
  other arithmetic  47.8 us (4%)
  starting transfers between devices  41 us (3%)
  between operations  18.7 us (1%)
  loops' own time  14.7 us (1%)
    gather x1536, local copies, waits for them, and re-layouts  1030 us
    psum x2, waiting for transfers between devices, broadcast(): return lax.psum(kept, axis)  73.6 us
    psum x2, waiting for transfers between devices, on_device(): totals = lax.psum(partial_value, 'ray')  72.5 us
    ppermute x8, starting transfers between devices, padded_2(): lax.ppermute(lax.slice_in_dim(block, block.shape[dim] - width, None, axis...  28 us
    ppermute x8, waiting for transfers between devices, padded_2(): lax.ppermute(lax.slice_in_dim(block, 0, width, axis=dim), axis, backward)  27.3 us
  transfers between devices with their start and end apart: 20, of which 16 were waited for; matrix products, arithmetic and copies ran while one was open for 0% of the time, Pallas kernels for 0%

commit v1 on v0

--- a/solution.py
+++ b/solution.py
@@ -146,7 +146,10 @@
         )
         padded = jnp.pad(current, ((0, 0), (0, 0), (margin, margin)))
         partial_value = project_block(padded, shifts, fraction, margin, breadth)
-        totals = lax.psum(partial_value, "ray")
+        size, totals = (lax.axis_size("ray"), partial_value)
+        for far in [1 << k for k in range(size.bit_length() - 1)]:
+            route = [(i_2, i_2 ^ far) for i_2 in range(size)]
+            totals = totals + lax.ppermute(totals, "ray", route)
         residual = broadcast(stored - totals, "ray", subset_slot)
         res_padded = jnp.pad(residual, ((0, 0), (0, 0), (margin, margin)))
         current = current + back_block(res_padded, shifts, fraction, margin, breadth) / (

time: 1360 us -> 1310 us (0.963)
  local copies, waits for them, and re-layouts: 1050 us -> 1020 us
  waiting for transfers between devices: 176 us -> 154 us
    psum x2 -> x0, waiting for transfers between devices: 72.5 us -> none  [on_device(): totals = lax.psum(partial_value, 'ray')]
    ppermute x0 -> x4, waiting for transfers between devices: none -> 50.7 us  [on_device(): totals = totals + lax.ppermute(totals, 'ray', route)]
    gather x1536, local copies, waits for them, and re-layouts: 1030 us -> 1000 us
  transfers between devices with their start and end apart: 20 -> 22, of which waited for: 16 -> 18; matrix products, arithmetic and copies ran while one was open for 0% -> 0% of each run, Pallas kernels for 0% -> 0%
where the time goes in v1:
time: 1310 us; the launch traced here: 1300 us
  local copies, waits for them, and re-layouts  1020 us (78%)
  waiting for transfers between devices  154 us (12%)
  other arithmetic  47.5 us (4%)
  starting transfers between devices  44.9 us (3%)
  between operations  18.5 us (1%)
  loops' own time  14.7 us (1%)
    gather x1536, local copies, waits for them, and re-layouts  1000 us
    psum x2, waiting for transfers between devices, broadcast(): return lax.psum(kept, axis)  74 us
    ppermute x4, waiting for transfers between devices, on_device(): totals = totals + lax.ppermute(totals, 'ray', route)  50.7 us
    ppermute x8, starting transfers between devices, padded_2(): lax.ppermute(lax.slice_in_dim(block, block.shape[dim] - width, None, axis...  28 us
    ppermute x8, waiting for transfers between devices, padded_2(): lax.ppermute(lax.slice_in_dim(block, 0, width, axis=dim), axis, backward)  27.3 us
  transfers between devices with their start and end apart: 22, of which 18 were waited for; matrix products, arithmetic and copies ran while one was open for 0% of the time, Pallas kernels for 0%

profile of v1, /device:TPU:1, one launch (start us, length us, event | category | flops | bytes accessed | tf_op | source)
XLA Modules:
  0.0 1296.9 jit_solution(6927985895491483402)
XLA Ops:
  14.1 267.2 %while.65 = (s32[]{:T(128)}, f32[16,2,2,4096]{3,2,1,0:T(2,128)S(1)}, f32[16,2,4]{2,1,0:T(2,128)S(1)}, f32[2,4,4116]{2,0,1:T(2,128)S(1)}, s32[16,2,4]{2,1,0:T(2,128)S(1)}, /*index=5*/s32[]{:T(128)}, s32[]{:T(128)}, s32[]{:T(128)}) while((s32[]{:T(128)}, f32[16,2,2,4096]{3,2,1,0:T(2,128)S(1)}, f32[16,2,4]{2,1,0:T(2,128)S(1)}, ...), condition=%wide.region_2.3_spmd, body=%wide.region_0.2_spmd.sunk | while | flops 245828 | bytes 789350 | solution.py:70
  14.2 16.1 %while.72 = (s32[]{:T(128)}, f32[4,2,4116]{2,1,0:T(2,128)S(1)}, s32[8,3]{0,1:T(4,128)S(1)}, f32[8,2,4097]{2,1,0:T(2,128)S(1)}, s32[]{:T(128)}) while((s32[]{:T(128)}, f32[4,2,4116]{2,1,0:T(2,128)S(1)}, s32[8,3]{0,1:T(4,128)S(1)}, f32[8,2,4097]{2,1,0:T(2,128)S(1)}, s32[]{:T(128)}) %tuple.255), condition=%wide.while_cond, body=%wide.while_body.sunk | while | flops 2 | bytes 67701 | solution.py:45
  30.9 16.1 %while.72 = (s32[]{:T(128)}, f32[4,2,4116]{2,1,0:T(2,128)S(1)}, s32[8,3]{0,1:T(4,128)S(1)}, f32[8,2,4097]{2,1,0:T(2,128)S(1)}, s32[]{:T(128)}) while((s32[]{:T(128)}, f32[4,2,4116]{2,1,0:T(2,128)S(1)}, s32[8,3]{0,1:T(4,128)S(1)}, f32[8,2,4097]{2,1,0:T(2,128)S(1)}, s32[]{:T(128)}) %tuple.255), condition=%wide.while_cond, body=%wide.while_body.sunk | while | flops 2 | bytes 67701 | solution.py:45
  47.6 16.1 %while.72 = (s32[]{:T(128)}, f32[4,2,4116]{2,1,0:T(2,128)S(1)}, s32[8,3]{0,1:T(4,128)S(1)}, f32[8,2,4097]{2,1,0:T(2,128)S(1)}, s32[]{:T(128)}) while((s32[]{:T(128)}, f32[4,2,4116]{2,1,0:T(2,128)S(1)}, s32[8,3]{0,1:T(4,128)S(1)}, f32[8,2,4097]{2,1,0:T(2,128)S(1)}, s32[]{:T(128)}) %tuple.255), condition=%wide.while_cond, body=%wide.while_body.sunk | while | flops 2 | bytes 67701 | solution.py:45
  64.3 16.1 %while.72 = (s32[]{:T(128)}, f32[4,2,4116]{2,1,0:T(2,128)S(1)}, s32[8,3]{0,1:T(4,128)S(1)}, f32[8,2,4097]{2,1,0:T(2,128)S(1)}, s32[]{:T(128)}) while((s32[]{:T(128)}, f32[4,2,4116]{2,1,0:T(2,128)S(1)}, s32[8,3]{0,1:T(4,128)S(1)}, f32[8,2,4097]{2,1,0:T(2,128)S(1)}, s32[]{:T(128)}) %tuple.255), condition=%wide.while_cond, body=%wide.while_body.sunk | while | flops 2 | bytes 67701 | solution.py:45
  81.0 16.1 %while.72 = (s32[]{:T(128)}, f32[4,2,4116]{2,1,0:T(2,128)S(1)}, s32[8,3]{0,1:T(4,128)S(1)}, f32[8,2,4097]{2,1,0:T(2,128)S(1)}, s32[]{:T(128)}) while((s32[]{:T(128)}, f32[4,2,4116]{2,1,0:T(2,128)S(1)}, s32[8,3]{0,1:T(4,128)S(1)}, f32[8,2,4097]{2,1,0:T(2,128)S(1)}, s32[]{:T(128)}) %tuple.255), condition=%wide.while_cond, body=%wide.while_body.sunk | while | flops 2 | bytes 67701 | solution.py:45
  97.7 16.1 %while.72 = (s32[]{:T(128)}, f32[4,2,4116]{2,1,0:T(2,128)S(1)}, s32[8,3]{0,1:T(4,128)S(1)}, f32[8,2,4097]{2,1,0:T(2,128)S(1)}, s32[]{:T(128)}) while((s32[]{:T(128)}, f32[4,2,4116]{2,1,0:T(2,128)S(1)}, s32[8,3]{0,1:T(4,128)S(1)}, f32[8,2,4097]{2,1,0:T(2,128)S(1)}, s32[]{:T(128)}) %tuple.255), condition=%wide.while_cond, body=%wide.while_body.sunk | while | flops 2 | bytes 67701 | solution.py:45
  114.4 16.1 %while.72 = (s32[]{:T(128)}, f32[4,2,4116]{2,1,0:T(2,128)S(1)}, s32[8,3]{0,1:T(4,128)S(1)}, f32[8,2,4097]{2,1,0:T(2,128)S(1)}, s32[]{:T(128)}) while((s32[]{:T(128)}, f32[4,2,4116]{2,1,0:T(2,128)S(1)}, s32[8,3]{0,1:T(4,128)S(1)}, f32[8,2,4097]{2,1,0:T(2,128)S(1)}, s32[]{:T(128)}) %tuple.255), condition=%wide.while_cond, body=%wide.while_body.sunk | while | flops 2 | bytes 67701 | solution.py:45
  131.1 16.1 %while.72 = (s32[]{:T(128)}, f32[4,2,4116]{2,1,0:T(2,128)S(1)}, s32[8,3]{0,1:T(4,128)S(1)}, f32[8,2,4097]{2,1,0:T(2,128)S(1)}, s32[]{:T(128)}) while((s32[]{:T(128)}, f32[4,2,4116]{2,1,0:T(2,128)S(1)}, s32[8,3]{0,1:T(4,128)S(1)}, f32[8,2,4097]{2,1,0:T(2,128)S(1)}, s32[]{:T(128)}) %tuple.255), condition=%wide.while_cond, body=%wide.while_body.sunk | while | flops 2 | bytes 67701 | solution.py:45
  147.8 16.1 %while.72 = (s32[]{:T(128)}, f32[4,2,4116]{2,1,0:T(2,128)S(1)}, s32[8,3]{0,1:T(4,128)S(1)}, f32[8,2,4097]{2,1,0:T(2,128)S(1)}, s32[]{:T(128)}) while((s32[]{:T(128)}, f32[4,2,4116]{2,1,0:T(2,128)S(1)}, s32[8,3]{0,1:T(4,128)S(1)}, f32[8,2,4097]{2,1,0:T(2,128)S(1)}, s32[]{:T(128)}) %tuple.255), condition=%wide.while_cond, body=%wide.while_body.sunk | while | flops 2 | bytes 67701 | solution.py:45
  164.5 16.1 %while.72 = (s32[]{:T(128)}, f32[4,2,4116]{2,1,0:T(2,128)S(1)}, s32[8,3]{0,1:T(4,128)S(1)}, f32[8,2,4097]{2,1,0:T(2,128)S(1)}, s32[]{:T(128)}) while((s32[]{:T(128)}, f32[4,2,4116]{2,1,0:T(2,128)S(1)}, s32[8,3]{0,1:T(4,128)S(1)}, f32[8,2,4097]{2,1,0:T(2,128)S(1)}, s32[]{:T(128)}) %tuple.255), condition=%wide.while_cond, body=%wide.while_body.sunk | while | flops 2 | bytes 67701 | solution.py:45
  181.2 16.1 %while.72 = (s32[]{:T(128)}, f32[4,2,4116]{2,1,0:T(2,128)S(1)}, s32[8,3]{0,1:T(4,128)S(1)}, f32[8,2,4097]{2,1,0:T(2,128)S(1)}, s32[]{:T(128)}) while((s32[]{:T(128)}, f32[4,2,4116]{2,1,0:T(2,128)S(1)}, s32[8,3]{0,1:T(4,128)S(1)}, f32[8,2,4097]{2,1,0:T(2,128)S(1)}, s32[]{:T(128)}) %tuple.255), condition=%wide.while_cond, body=%wide.while_body.sunk | while | flops 2 | bytes 67701 | solution.py:45
  197.9 16.1 %while.72 = (s32[]{:T(128)}, f32[4,2,4116]{2,1,0:T(2,128)S(1)}, s32[8,3]{0,1:T(4,128)S(1)}, f32[8,2,4097]{2,1,0:T(2,128)S(1)}, s32[]{:T(128)}) while((s32[]{:T(128)}, f32[4,2,4116]{2,1,0:T(2,128)S(1)}, s32[8,3]{0,1:T(4,128)S(1)}, f32[8,2,4097]{2,1,0:T(2,128)S(1)}, s32[]{:T(128)}) %tuple.255), condition=%wide.while_cond, body=%wide.while_body.sunk | while | flops 2 | bytes 67701 | solution.py:45
  214.6 16.1 %while.72 = (s32[]{:T(128)}, f32[4,2,4116]{2,1,0:T(2,128)S(1)}, s32[8,3]{0,1:T(4,128)S(1)}, f32[8,2,4097]{2,1,0:T(2,128)S(1)}, s32[]{:T(128)}) while((s32[]{:T(128)}, f32[4,2,4116]{2,1,0:T(2,128)S(1)}, s32[8,3]{0,1:T(4,128)S(1)}, f32[8,2,4097]{2,1,0:T(2,128)S(1)}, s32[]{:T(128)}) %tuple.255), condition=%wide.while_cond, body=%wide.while_body.sunk | while | flops 2 | bytes 67701 | solution.py:45
  231.3 16.1 %while.72 = (s32[]{:T(128)}, f32[4,2,4116]{2,1,0:T(2,128)S(1)}, s32[8,3]{0,1:T(4,128)S(1)}, f32[8,2,4097]{2,1,0:T(2,128)S(1)}, s32[]{:T(128)}) while((s32[]{:T(128)}, f32[4,2,4116]{2,1,0:T(2,128)S(1)}, s32[8,3]{0,1:T(4,128)S(1)}, f32[8,2,4097]{2,1,0:T(2,128)S(1)}, s32[]{:T(128)}) %tuple.255), condition=%wide.while_cond, body=%wide.while_body.sunk | while | flops 2 | bytes 67701 | solution.py:45
  248.0 16.1 %while.72 = (s32[]{:T(128)}, f32[4,2,4116]{2,1,0:T(2,128)S(1)}, s32[8,3]{0,1:T(4,128)S(1)}, f32[8,2,4097]{2,1,0:T(2,128)S(1)}, s32[]{:T(128)}) while((s32[]{:T(128)}, f32[4,2,4116]{2,1,0:T(2,128)S(1)}, s32[8,3]{0,1:T(4,128)S(1)}, f32[8,2,4097]{2,1,0:T(2,128)S(1)}, s32[]{:T(128)}) %tuple.255), condition=%wide.while_cond, body=%wide.while_body.sunk | while | flops 2 | bytes 67701 | solution.py:45
  264.7 16.1 %while.72 = (s32[]{:T(128)}, f32[4,2,4116]{2,1,0:T(2,128)S(1)}, s32[8,3]{0,1:T(4,128)S(1)}, f32[8,2,4097]{2,1,0:T(2,128)S(1)}, s32[]{:T(128)}) while((s32[]{:T(128)}, f32[4,2,4116]{2,1,0:T(2,128)S(1)}, s32[8,3]{0,1:T(4,128)S(1)}, f32[8,2,4097]{2,1,0:T(2,128)S(1)}, s32[]{:T(128)}) %tuple.255), condition=%wide.while_cond, body=%wide.while_body.sunk | while | flops 2 | bytes 67701 | solution.py:45
  287.7 22.5 %collective-permute-done.1 = f32[32,2,4096]{2,1,0:T(2,128)S(1)} collective-permute-done((f32[32,2,4096]{2,1,0:T(2,128)S(1)}, f32[32,2,4096]{2,1,0:T(2,128)S(1)}, u32[]{:S(2)}, u32[]{:S(2)}) %collective-permute-start.1) | collective-permute-done | bytes 1048608 | tf_op jit(solution)/shard_map/ppermute | solution.py:152
  312.6 37.6 %all-reduce.19.cloned.1.call-done = f32[32,2,4096]{2,1,0:T(2,128)} async-done(((f32[32,2,4096]{2,1,0:T(2,128)}), f32[32,2,4096]{2,1,0:T(2,128)}) %all-reduce.19.cloned.1.call-update) | async-done | bytes 1048592 | tf_op jit(solution)/shard_map/psum | solution.py:16
  352.7 264.7 %while.69 = (s32[]{:T(128)}, f32[2,4,4096]{2,0,1:T(2,128)S(1)}, f32[16,2,4]{2,1,0:T(2,128)S(1)}, f32[16,2,2,4116]{3,2,1,0:T(2,128)S(1)}, s32[16,2,4]{2,1,0:T(2,128)S(1)}, /*index=5*/s32[]{:T(128)}, s32[]{:T(128)}, s32[]{:T(128)}) while((s32[]{:T(128)}, f32[2,4,4096]{2,0,1:T(2,128)S(1)}, f32[16,2,4]{2,1,0:T(2,128)S(1)}, ...), condition=%wide.region_6.7_spmd.clone, body=%wide.region_4.6_spmd.clone.sunk | while | flops 294981 | bytes 1248752 | solution.py:92
  656.4 261.2 %while.67 = (s32[]{:T(128)}, f32[16,2,2,4096]{3,2,1,0:T(2,128)S(1)}, f32[16,2,4]{2,1,0:T(2,128)S(1)}, f32[2,4,4116]{2,0,1:T(2,128)S(1)}, s32[16,2,4]{2,1,0:T(2,128)S(1)}, /*index=5*/s32[]{:T(128)}, s32[]{:T(128)}, s32[]{:T(128)}) while((s32[]{:T(128)}, f32[16,2,2,4096]{3,2,1,0:T(2,128)S(1)}, f32[16,2,4]{2,1,0:T(2,128)S(1)}, ...), condition=%wide.region_9.10_spmd, body=%wide.region_7.9_spmd.sunk | while | flops 245828 | bytes 789350 | solution.py:70
  922.7 22.9 %collective-permute-done.11 = f32[32,2,4096]{2,1,0:T(2,128)S(1)} collective-permute-done((f32[32,2,4096]{2,1,0:T(2,128)S(1)}, f32[32,2,4096]{2,1,0:T(2,128)S(1)}, u32[]{:S(2)}, u32[]{:S(2)}) %collective-permute-start.11) | collective-permute-done | bytes 1048608 | tf_op jit(solution)/shard_map/ppermute | solution.py:152
  947.8 36.4 %all-reduce.21.cloned.1.call-done = f32[32,2,4096]{2,1,0:T(2,128)} async-done(((f32[32,2,4096]{2,1,0:T(2,128)}), f32[32,2,4096]{2,1,0:T(2,128)}) %all-reduce.21.cloned.1.call-update) | async-done | bytes 1048592 | tf_op jit(solution)/shard_map/psum | solution.py:16
  986.5 264.7 %while.71 = (s32[]{:T(128)}, f32[2,4,4096]{2,0,1:T(2,128)S(1)}, f32[16,2,4]{2,1,0:T(2,128)S(1)}, f32[16,2,2,4116]{3,2,1,0:T(2,128)S(1)}, s32[16,2,4]{2,1,0:T(2,128)S(1)}, /*index=5*/s32[]{:T(128)}, s32[]{:T(128)}, s32[]{:T(128)}) while((s32[]{:T(128)}, f32[2,4,4096]{2,0,1:T(2,128)S(1)}, f32[16,2,4]{2,1,0:T(2,128)S(1)}, ...), condition=%wide.region_13.14_spmd.clone, body=%wide.region_11.13_spmd.clone.sunk | while | flops 294981 | bytes 1248752 | solution.py:92
  (2238 shorter events, 1898.5 us)
Async XLA Ops:
  6.5 343.7 %all-reduce.19.cloned.1.call-start = ((), (), s32[]{:S(2)}) async-start(), calls=%async_computation | async-start | bytes 2097152 | tf_op jit(solution)/shard_map/psum | solution.py:16
  281.3 29.0 %copy-start = (f32[1,32,2,4096]{3,2,1,0:T(2,128)S(1)}, f32[1,32,2,4096]{3,2,1,0:T(2,128)}, u32[]{:S(2)}) copy-start(f32[1,32,2,4096]{3,2,1,0:T(2,128)} %param.13) | copy-start | bytes 3145732
  281.3 2.7 collective-permute-start
  284.7 25.6 %collective-permute-start.1 = (f32[32,2,4096]{2,1,0:T(2,128)S(1)}, f32[32,2,4096]{2,1,0:T(2,128)S(1)}, u32[]{:S(2)}, u32[]{:S(2)}) collective-permute-start(f32[32,2,4096]{2,1,0:T(2,128)S(1)} %bitcast_add_fusion.1), channel_id=1, source_target_pairs={{0,16},{8,24},{16,0},{24,8},{1,17},{9,25},{17,1},{25,9},{2,18},{10... | collective-permute-start | bytes 3145736 | tf_op jit(solution)/shard_map/ppermute | solution.py:152
  312.4 671.7 %all-reduce.21.cloned.1.call-start = ((), (), s32[]{:S(2)}) async-start(), calls=%async_computation.1 | async-start | bytes 2097152 | tf_op jit(solution)/shard_map/psum | solution.py:16
  352.6 264.8 %copy-start.1 = (f32[2,4,4096]{2,1,0:T(4,128)S(1)}, f32[2,4,4096]{2,1,0:T(4,128)}, u32[]{:S(2)}) copy-start(f32[2,4,4096]{2,1,0:T(4,128)} %param.12) | copy-start | bytes 393220
  617.6 5.6 collective-permute-start.2
  621.2 5.2 collective-permute-start.3
  626.5 5.0 collective-permute-start.4
  629.6 5.7 collective-permute-start.5
  636.3 5.3 collective-permute-start.6
  639.6 5.2 collective-permute-start.7
  645.0 5.9 collective-permute-start.8
  649.0 5.7 collective-permute-start.9
  917.6 2.7 collective-permute-start.10
  920.9 24.6 %collective-permute-start.11 = (f32[32,2,4096]{2,1,0:T(2,128)S(1)}, f32[32,2,4096]{2,1,0:T(2,128)S(1)}, u32[]{:S(2)}, u32[]{:S(2)}) collective-permute-start(f32[32,2,4096]{2,1,0:T(2,128)S(1)} %bitcast_add_fusion), channel_id=1, source_target_pairs={{0,16},{8,24},{16,0},{24,8},{1,17},{9,25},{17,1},{25,9},{2,18},{10... | collective-permute-start | bytes 3145736 | tf_op jit(solution)/shard_map/ppermute | solution.py:152
  1251.4 5.5 collective-permute-start.12
  1255.0 5.2 collective-permute-start.13
  1260.4 5.0 collective-permute-start.14
  1263.5 5.7 collective-permute-start.15
  1270.1 5.3 collective-permute-start.16
  1273.5 5.2 collective-permute-start.17
  1278.8 5.9 collective-permute-start.18
  1282.8 5.7 collective-permute-start.19
Sparse Core Ops, SparseCore 0:
  312.5 37.6 all-reduce.18
  947.9 36.2 all-reduce.20
